TPU v7x, 32 devices: a whole 2x2x4 slice. The times are simulated.
32 devices in a mesh: dp: 2 (over y), seq: 16 (over z, x, core).
Axes of the slice: x: 2, y: 2, z: 4, core: 2. Of those that a mesh axis runs over, the one named last changes fastest.
Arguments:
- layer_input: bfloat16 [4096, 1024], P(('dp', 'seq')), may hold values from -6 to 6
- norm_gain: bfloat16 [1024], P('dp'), may hold values from 0.5 to 1.5
- in_weight: bfloat16 [1024, 4384], P('dp'), may hold values from -0.1875 to 0.1875
- conv_weight: bfloat16 [4, 2304], P(None, 'dp'), may hold values from -3 to 3
- conv_bias: bfloat16 [2304], P('dp'), may hold values from -2 to 2
- step_bias: bfloat16 [32], P('dp'), may hold values from -5 to -1
- rate_log: bfloat16 [32], P('dp'), may hold values from -4 to 2
- skip_gain: bfloat16 [32], P('dp'), may hold values from 0.5 to 2
- gate_gain: bfloat16 [2048], P('dp'), may hold values from 0.5 to 1.5
- out_weight: bfloat16 [2048, 1024], P('dp'), may hold values from -0.125 to 0.125
- cotangent: bfloat16 [4096, 1024], P(('dp', 'seq')), may hold values from -6 to 6
Outputs:
- layer_output: bfloat16 [4096, 1024], P(('dp', 'seq'))
- input_grad: float32 [4096, 1024], P(('dp', 'seq'))
- norm_gain_grad: float32 [1024], P('dp')
- in_weight_grad: float32 [1024, 4384], P('dp')
- conv_weight_grad: float32 [4, 2304], P(None, 'dp')
- conv_bias_grad: float32 [2304], P('dp')
- step_bias_grad: float32 [32], P('dp')
- rate_log_grad: float32 [32], P('dp')
- skip_gain_grad: float32 [32], P('dp')
- gate_gain_grad: float32 [2048], P('dp')
- out_weight_grad: float32 [2048, 1024], P('dp')
All inputs are finite; a program needn't handle non-finite values.
Results may differ from a plain program's by a relative error of at most 0.012.
Values may be sent and summed in bfloat16 or wider, within the bound.
No kernel may reach another device: no remote copies, remote signals or barrier semaphores. Data moves between devices by JAX's collectives and lax.ppermute only.
A program may use at most 192 MiB of HBM per device.

v0:
```python
import jax
import jax.numpy as jnp
from jax import lax
from jax.sharding import PartitionSpec as P

BLOCK = 256
epsilon = 1e-05
highest = lax.Precision.HIGHEST


def front_norm(values, gain):
    scale = lax.rsqrt(jnp.mean(values * values, axis=-1, keepdims=True) + epsilon)
    return values * scale * gain


def gated_norm(mixer_out, gate_in, gain):
    gated = mixer_out * jax.nn.silu(gate_in)
    scale = lax.rsqrt(jnp.mean(gated * gated, axis=-1, keepdims=True) + epsilon)
    return gated * scale * gain


def causal_conv(values, taps, offset):
    width = taps.shape[0]
    length = values.shape[0]
    padded = jnp.concatenate(
        [jnp.zeros((width - 1, values.shape[1]), values.dtype), values], axis=0
    )
    total = offset[None, :] + jnp.zeros_like(values)
    for index in range(width):
        total = total + taps[index][None, :] * padded[index : index + length]
    return jax.nn.silu(total)


def scan_blocks(values, steps, rates, keys, queries):
    length, heads, hdim = values.shape
    states = keys.shape[1]
    blocks = length // BLOCK
    items = (
        values.reshape(blocks, BLOCK, heads, hdim),
        steps.reshape(blocks, BLOCK, heads),
        keys.reshape(blocks, BLOCK, states),
        queries.reshape(blocks, BLOCK, states),
    )

    def one_block(state, item):
        val_blk, step_blk, key_blk, query_blk = item
        logs = (step_blk * rates[None, :]).T
        cums = jnp.cumsum(logs, axis=1)
        rows = lax.broadcasted_iota(jnp.int32, (BLOCK, BLOCK), 0)
        cols = lax.broadcasted_iota(jnp.int32, (BLOCK, BLOCK), 1)
        lower = (rows >= cols)[None]
        spread = cums[:, :, None] - cums[:, None, :]
        decay = jnp.where(lower, jnp.exp(jnp.where(lower, spread, 0.0)), 0.0)
        scores = jnp.dot(query_blk, key_blk.T, precision=highest)
        weights = scores[None] * decay * step_blk.T[:, None, :]
        inside = jnp.einsum("hts,shp->thp", weights, val_blk, precision=highest)
        carried = (
            jnp.einsum("tn,hpn->thp", query_blk, state, precision=highest)
            * jnp.exp(cums).T[:, :, None]
        )
        tail = jnp.exp(cums[:, -1:] - cums) * step_blk.T
        update = jnp.einsum("hs,shp,sn->hpn", tail, val_blk, key_blk, precision=highest)
        fresh = state * jnp.exp(cums[:, -1])[:, None, None] + update
        return (fresh, inside + carried)

    start = jnp.zeros((heads, hdim, states), jnp.float32)
    final_state, outputs = lax.scan(jax.checkpoint(one_block), start, items)
    return outputs.reshape(length, heads, hdim)


def mixer(
    x_head, step_raw, key_query, x_taps, x_offset, kq_taps, kq_offset, step_shift, rate_logs, skips
):
    x_conv = causal_conv(x_head, x_taps, x_offset)
    kq_conv = causal_conv(key_query, kq_taps, kq_offset)
    states = kq_conv.shape[1] // 2
    keys = kq_conv[:, :states]
    queries = kq_conv[:, states:]
    steps = jax.nn.softplus(step_raw + step_shift[None, :])
    rates = -jnp.exp(rate_logs)
    heads = step_shift.shape[0]
    length = x_head.shape[0]
    values = x_conv.reshape(length, heads, -1)
    mixed = scan_blocks(values, steps, rates, keys, queries) + values * skips[None, :, None]
    return mixed.reshape(length, -1)


def own_block(values, dim):
    parts = lax.axis_size("dp")
    width = values.shape[dim] // parts
    return lax.dynamic_slice_in_dim(values, lax.axis_index("dp") * width, width, dim)


def local(
    layer_input,
    norm_gain,
    in_weight,
    conv_weight,
    conv_bias,
    step_bias,
    rate_log,
    skip_gain,
    gate_gain,
    out_weight,
    cotangent,
):
    (
        full_gain,
        full_in,
        full_taps,
        full_offset,
        full_shift,
        full_rates,
        full_skip,
        full_gate,
        full_out,
    ) = (
        lax.all_gather(norm_gain, "dp", axis=0, tiled=True),
        lax.all_gather(in_weight, "dp", axis=0, tiled=True),
        lax.all_gather(conv_weight, "dp", axis=1, tiled=True),
        lax.all_gather(conv_bias, "dp", axis=0, tiled=True),
        lax.all_gather(step_bias, "dp", axis=0, tiled=True),
        lax.all_gather(rate_log, "dp", axis=0, tiled=True),
        lax.all_gather(skip_gain, "dp", axis=0, tiled=True),
        lax.all_gather(gate_gain, "dp", axis=0, tiled=True),
        lax.all_gather(out_weight, "dp", axis=0, tiled=True),
    )
    inner = full_out.shape[0]
    heads = full_shift.shape[0]
    states = (full_taps.shape[1] - inner) // 2
    group = lax.axis_size("seq")
    local_heads = heads // group
    span = local_heads * (inner // heads)
    rank = lax.axis_index("seq")
    tok_vals = layer_input.astype(jnp.float32)
    normed, pull_front = jax.vjp(front_norm, tok_vals, full_gain.astype(jnp.float32))
    normed_low = normed.astype(jnp.bfloat16)
    proj_low = jnp.dot(normed_low, full_in, preferred_element_type=jnp.float32).astype(jnp.bfloat16)
    gate_in = proj_low[:, :inner]
    x_part = proj_low[:, inner : 2 * inner]
    kq_part = proj_low[:, 2 * inner : 2 * inner + 2 * states]
    step_part = proj_low[:, 2 * inner + 2 * states :]
    x_head, step_head = (
        lax.all_to_all(x_part, "seq", split_axis=1, concat_axis=0, tiled=True),
        lax.all_to_all(step_part, "seq", split_axis=1, concat_axis=0, tiled=True),
    )
    kq_whole = lax.all_gather(kq_part, "seq", axis=0, tiled=True)
    taps_f = full_taps.astype(jnp.float32)
    offset_f = full_offset.astype(jnp.float32)
    x_taps = lax.dynamic_slice_in_dim(taps_f, rank * span, span, 1)
    x_offset = lax.dynamic_slice_in_dim(offset_f, rank * span, span, 0)
    shift_own = lax.dynamic_slice_in_dim(
        full_shift.astype(jnp.float32), rank * local_heads, local_heads, 0
    )
    rates_own = lax.dynamic_slice_in_dim(
        full_rates.astype(jnp.float32), rank * local_heads, local_heads, 0
    )
    skip_own = lax.dynamic_slice_in_dim(
        full_skip.astype(jnp.float32), rank * local_heads, local_heads, 0
    )
    mixed, pull_mix = jax.vjp(
        mixer,
        x_head.astype(jnp.float32),
        step_head.astype(jnp.float32),
        kq_whole.astype(jnp.float32),
        x_taps,
        x_offset,
        taps_f[:, inner:],
        offset_f[inner:],
        shift_own,
        rates_own,
        skip_own,
    )
    mixer_tok = lax.all_to_all(
        mixed.astype(jnp.bfloat16), "seq", split_axis=0, concat_axis=1, tiled=True
    )
    gate_out, pull_gate = jax.vjp(
        gated_norm,
        mixer_tok.astype(jnp.float32),
        gate_in.astype(jnp.float32),
        full_gate.astype(jnp.float32),
    )
    gate_low = gate_out.astype(jnp.bfloat16)
    layer_output = (
        tok_vals + jnp.dot(gate_low, full_out, preferred_element_type=jnp.float32)
    ).astype(jnp.bfloat16)
    out_grad = jnp.dot(gate_low.T, cotangent, preferred_element_type=jnp.float32)
    d_gate_out = jnp.dot(cotangent, full_out.T, preferred_element_type=jnp.float32)
    d_mixer_tok, d_gate_in, gate_grad = pull_gate(d_gate_out)
    d_mixer_head = lax.all_to_all(
        d_mixer_tok.astype(jnp.bfloat16), "seq", split_axis=1, concat_axis=0, tiled=True
    )
    (
        d_x_head,
        d_step_head,
        d_kq_whole,
        d_x_taps,
        d_x_offset,
        d_kq_taps,
        d_kq_offset,
        d_shift_own,
        d_rates_own,
        d_skip_own,
    ) = pull_mix(d_mixer_head.astype(jnp.float32))
    d_x_tok, d_step_tok = (
        lax.all_to_all(
            d_x_head.astype(jnp.bfloat16), "seq", split_axis=0, concat_axis=1, tiled=True
        ),
        lax.all_to_all(
            d_step_head.astype(jnp.bfloat16), "seq", split_axis=0, concat_axis=1, tiled=True
        ),
    )
    d_kq_tok = lax.psum_scatter(
        d_kq_whole.astype(jnp.bfloat16), "seq", scatter_dimension=0, tiled=True
    )
    d_proj = jnp.concatenate(
        [d_gate_in.astype(jnp.bfloat16), d_x_tok, d_kq_tok, d_step_tok], axis=1
    )
    in_grad = jnp.dot(normed_low.T, d_proj, preferred_element_type=jnp.float32)
    d_normed = jnp.dot(d_proj, full_in.T, preferred_element_type=jnp.float32)
    d_front, gain_grad = pull_front(d_normed)
    input_grad = d_front + cotangent.astype(jnp.float32)
    x_tap_grad = lax.dynamic_update_slice_in_dim(
        jnp.zeros((taps_f.shape[0], inner), jnp.float32), d_x_taps, rank * span, 1
    )
    taps_grad = jnp.concatenate([x_tap_grad, d_kq_taps], axis=1)
    x_off_grad = lax.dynamic_update_slice_in_dim(
        jnp.zeros((inner,), jnp.float32), d_x_offset, rank * span, 0
    )
    offset_grad = jnp.concatenate([x_off_grad, d_kq_offset], axis=0)
    head_zeros = jnp.zeros((heads,), jnp.float32)
    shift_grad = lax.dynamic_update_slice_in_dim(head_zeros, d_shift_own, rank * local_heads, 0)
    rates_grad = lax.dynamic_update_slice_in_dim(head_zeros, d_rates_own, rank * local_heads, 0)
    skip_grad = lax.dynamic_update_slice_in_dim(head_zeros, d_skip_own, rank * local_heads, 0)
    in_part, out_part = (
        lax.psum_scatter(in_grad, ("dp", "seq"), scatter_dimension=0, tiled=True),
        lax.psum_scatter(out_grad, ("dp", "seq"), scatter_dimension=0, tiled=True),
    )
    in_shard, out_shard = (
        lax.all_gather(in_part, "seq", axis=0, tiled=True),
        lax.all_gather(out_part, "seq", axis=0, tiled=True),
    )
    gain_all, taps_all, offset_all, shift_all, rates_all, skip_all, gate_all = lax.psum(
        (gain_grad, taps_grad, offset_grad, shift_grad, rates_grad, skip_grad, gate_grad),
        ("dp", "seq"),
    )
    gain_shard = own_block(gain_all, 0)
    taps_shard = own_block(taps_all, 1)
    offset_shard = own_block(offset_all, 0)
    shift_shard = own_block(shift_all, 0)
    rates_shard = own_block(rates_all, 0)
    skip_shard = own_block(skip_all, 0)
    gate_shard = own_block(gate_all, 0)
    return (
        layer_output,
        input_grad,
        gain_shard,
        in_shard,
        taps_shard,
        offset_shard,
        shift_shard,
        rates_shard,
        skip_shard,
        gate_shard,
        out_shard,
    )


def solution(mesh):
    return jax.shard_map(
        local,
        mesh=mesh,
        in_specs=(
            P(("dp", "seq"), None),
            P("dp"),
            P("dp", None),
            P(None, "dp"),
            P("dp"),
            P("dp"),
            P("dp"),
            P("dp"),
            P("dp"),
            P("dp", None),
            P(("dp", "seq"), None),
        ),
        out_specs=(
            P(("dp", "seq"), None),
            P(("dp", "seq"), None),
            P("dp"),
            P("dp", None),
            P(None, "dp"),
            P("dp"),
            P("dp"),
            P("dp"),
            P("dp"),
            P("dp"),
            P("dp", None),
        ),
        check_vma=False,
    )
```

profile of v0, /device:TPU:0, one launch (start us, length us, event | category | flops | bytes accessed | tf_op | source)
XLA Modules:
  0.0 1092.6 jit_solution(7979534498139653313)
XLA Ops:
  8.0 5.3 all-gather
  13.4 111.9 %all-gather.8.cloned.1.call-done = bf16[1024,4384]{0,1:T(8,128)(2,1)} async-done(((bf16[512,4384]{0,1:T(8,128)(2,1)}), bf16[1024,4384]{0,1:T(8,128)(2,1)}) %all-gather.8.cloned.1.call-update) | async-done | bytes 8978448 | tf_op jit(solution)/shard_map/all_gather | solution.py:119
  125.3 6.1 convolution_convert_fusion
  133.0 4.3 all-gather.1
  137.9 5.6 all-to-all-start
  145.6 4.9 all-reduce.26
  150.5 4.4 all_gather.41
  157.2 6.5 all-to-all-start.1
  165.2 12.9 %all-to-all-done.1 = bf16[128,16,128]{2,0,1:T(8,128)(2,1)S(1)} async-done(((bf16[128,16,128]{2,0,1:T(8,128)(2,1)}), bf16[128,16,128]{2,0,1:T(8,128)(2,1)S(1)}, u32[]{:S(2)}, u32[]{:S(2)}) %all-to-all-start.1) | async-done | bytes 524320 | tf_op jit(solution)/shard_map/all_to_all | solution.py:144
  185.9 3.1 fusion.89
  192.1 2.7 copy.149
  195.8 75.2 %while.44 = (s32[]{:T(128)}, f32[2,64,128]{2,1,0:T(8,128)S(1)}, f32[8,256,2,64]{1,3,2,0:T(8,128)}, f32[8,2,64,128]{3,2,1,0:T(8,128)}, f32[8,256,2]{1,2,0:T(2,128...) while((s32[]{:T(128)}, f32[2,64,128]{2,1,0:T(8,128)S(1)}, ...), condition=%wide.region_4.5_spmd.clone.clone, body=%wide.region_1.4_spmd.clone.clone.sunk | while | flops 302892544 | bytes 2142528 | solution.py:67
  271.0 3.9 copy.138
  275.0 3.3 reshape.488
  280.5 5.1 all-to-all-start.2
  285.6 4.3 all_gather.44
  289.9 10.1 all-to-all-done.2
  302.0 4.2 multiply_reduce_fusion.8
  306.2 2.9 fusion.96
  311.2 4.1 all-to-all-start.3
  316.2 13.6 %all-to-all-done.3 = bf16[128,16,128]{2,0,1:T(8,128)(2,1)S(1)} async-done(((bf16[128,16,128]{2,0,1:T(8,128)(2,1)}), bf16[128,16,128]{2,0,1:T(8,128)(2,1)S(1)}, u32[]{:S(2)}, u32[]{:S(2)}) %all-to-all-start.3) | async-done | bytes 524320 | tf_op jit(solution)/shard_map/all_to_all | solution.py:190
  330.9 3.3 reshape.489
  334.3 3.9 copy.123
  342.0 173.5 %while.43 = (s32[]{:T(128)}, f32[2]{0:T(128)}, f32[2,64,128]{2,1,0:T(8,128)S(1)}, f32[8,256,2,64]{1,3,2,0:T(8,128)}, f32[8,256,2]{1,2,0:T(2,128)}, /*index=5*/f3...) while((s32[]{:T(128)}, f32[2]{0:T(128)}, ...), condition=%wide.region_20.21_spmd.clone, body=%wide.region_7.20_spmd.clone.sunk | while | flops 758179328 | bytes 7921532 | solution.py:67
  351.7 2.5 reduce-window.74
  373.4 2.5 reduce-window.74
  395.1 2.5 reduce-window.74
  416.8 2.5 reduce-window.74
  438.5 2.5 reduce-window.74
  460.2 2.5 reduce-window.74
  515.5 2.7 copy.143
  520.8 4.7 multiply_reduce_fusion.6
  529.4 4.7 fusion.131
  537.6 3.5 reshape.490
  541.2 3.5 multiply_reduce_fusion.11
  546.2 4.3 all-to-all-start.4
  551.2 16.4 %all-to-all-done.4 = bf16[16,128,128]{2,1,0:T(8,128)(2,1)S(1)} async-done(((bf16[16,128,128]{2,1,0:T(8,128)(2,1)}), bf16[16,128,128]{2,1,0:T(8,128)(2,1)S(1)}, u32[]{:S(2)}, u32[]{:S(2)}) %all-to-all-start.4) | async-done | bytes 524320 | tf_op jit(solution)/shard_map/all_to_all | solution.py:206
  567.6 5.3 all-to-all-start.5
  573.3 13.9 %reduce-scatter.10.cloned.1.call-done = bf16[128,256]{1,0:T(8,128)(2,1)} async-done(((bf16[2048,256]{1,0:T(8,128)(2,1)}), bf16[128,256]{1,0:T(8,128)(2,1)}) %reduce-scatter.10.cloned.1.call-update) | async-done | bytes 65552
  588.2 8.0 fusion.110
  596.2 141.3 %reduce-scatter.8.cloned.1.call-done = f32[64,1024]{1,0:T(8,128)} async-done(((f32[2048,1024]{1,0:T(8,128)}), f32[64,1024]{1,0:T(8,128)}) %reduce-scatter.8.cloned.1.call-update) | async-done | bytes 262160 | tf_op jit(solution)/shard_map/reduce_scatter | solution.py:237
  737.6 194.8 %reduce-scatter.6.cloned.1.call-done = f32[32,4384]{1,0:T(8,128)} async-done(((f32[1024,4384]{1,0:T(8,128)}), f32[32,4384]{1,0:T(8,128)}) %reduce-scatter.6.cloned.1.call-update) | async-done | bytes 561168 | tf_op jit(solution)/shard_map/reduce_scatter | solution.py:236
  932.6 4.1 fusion.90
  938.3 5.1 fusion.106
  943.4 47.0 %all-reduce.25 = (f32[1024]{0:T(1024)S(1)}, f32[4,2304]{1,0:T(4,128)S(1)}, f32[2304]{0:T(1024)S(1)}, f32[32]{0:T(128)S(1)}, f32[32]{0:T(128)S(1)}, /*index=5*/f32[32]{0:T(128)S(1)}, f32[2048]{0:T(1024)S(1)}) all-reduce(f32[1024]{0:T(1024)S(1)} %get-tuple-element.697, ...), channel_id=1, replica_groups=mesh['dp'=2,'seq'=16] {'dp','seq'}, use_global_device_ids=true, to_apply=%region_24.25 | all-reduce | flops 14688 | bytes 117504 | tf_op jit(solution)/shard_map/psum | solution.py:243
  995.8 75.6 %all-gather.14.cloned.1.call-done = f32[512,4384]{1,0:T(8,128)} async-done(((f32[32,4384]{1,0:T(8,128)}), f32[512,4384]{1,0:T(8,128)}) %all-gather.14.cloned.1.call-update) | async-done | bytes 8978448 | tf_op jit(solution)/shard_map/all_gather | solution.py:240
  1071.4 9.4 copy.130
  1080.8 4.8 copy.253
  (786 shorter events, 284.4 us)
Async XLA Ops:
  7.2 118.1 %all-gather.8.cloned.1.call-start = ((), (), s32[]{:S(2)}) async-start(), calls=%async_computation.9 | async-start | bytes 13467648 | tf_op jit(solution)/shard_map/all_gather | solution.py:119
  7.9 176.3 %all-gather.10.cloned.1.call-start = ((), (), s32[]{:S(2)}) async-start(), calls=%async_computation.10 | async-start | bytes 1114112 | tf_op jit(solution)/shard_map/all_gather | solution.py:147
  13.4 118.0 %copy-start.65 = (f32[128]{0:T(128)}, f32[128]{0:T(128)S(1)}, u32[]{:S(2)}) copy-start(f32[128]{0:T(128)S(1)} %fusion.108) | copy-start | bytes 1540
  13.4 118.0 %copy-start.27 = (f32[128]{0:T(128)}, f32[128]{0:T(128)S(1)}, u32[]{:S(2)}) copy-start(f32[128]{0:T(128)S(1)} %fusion.126) | copy-start | bytes 1540
  131.5 25.7 %copy-start.7 = (bf16[128,4384]{0,1:T(8,128)(2,1)}, bf16[128,4384]{0,1:T(8,128)(2,1)S(1)}, u32[]{:S(2)}) copy-start(bf16[128,4384]{0,1:T(8,128)(2,1)S(1)} %convolution_convert_fusion) | copy-start | bytes 3366916
  131.5 12.1 %copy-start.75 = (u32[32]{0:T(128)S(1)}, u32[32]{0:T(128)}, u32[]{:S(2)}) copy-start(u32[32]{0:T(128)} %constant.205) | copy-start | bytes 388
  131.5 13.4 %copy-start.72 = (bf16[16]{0:T(256)(128)(2,1)S(1)}, bf16[16]{0:T(256)(128)(2,1)}, u32[]{:S(2)}) copy-start(bf16[16]{0:T(256)(128)(2,1)} %param.20) | copy-start | bytes 100
  131.5 13.6 %copy-start.73 = (bf16[16]{0:T(256)(128)(2,1)S(1)}, bf16[16]{0:T(256)(128)(2,1)}, u32[]{:S(2)}) copy-start(bf16[16]{0:T(256)(128)(2,1)} %param.22) | copy-start | bytes 100
  131.5 13.8 %copy-start.74 = (bf16[16]{0:T(256)(128)(2,1)S(1)}, bf16[16]{0:T(256)(128)(2,1)}, u32[]{:S(2)}) copy-start(bf16[16]{0:T(256)(128)(2,1)} %param.21) | copy-start | bytes 100
  131.5 19.0 %copy-start.43 = (bf16[4,1152]{1,0:T(4,128)(2,1)S(1)}, bf16[4,1152]{1,0:T(4,128)(2,1)}, u32[]{:S(2)}) copy-start(bf16[4,1152]{1,0:T(4,128)(2,1)} %param.18) | copy-start | bytes 27652
  132.2 169.8 %all-gather.12.cloned.1.call-start = ((), (), s32[]{:S(2)}) async-start(), calls=%async_computation.11 | async-start | bytes 6291456 | tf_op jit(solution)/shard_map/all_gather | solution.py:126
  137.9 19.3 %all-to-all-start = ((bf16[128,16,2]{0,2,1:T(2,128)(2,1)}), bf16[128,16,2]{0,2,1:T(2,128)(2,1)S(1)}, u32[]{:S(2)}, u32[]{:S(2)}) async-start(bf16[128,16,2]{0,2,1:T(2,128)(2,1)} %bitcast.3), calls=%async_computation | async-start | bytes 16384 | tf_op jit(solution)/shard_map/all_to_all | solution.py:145
  150.5 27.7 %copy-start.69 = (f32[32]{0:T(128)}, f32[32]{0:T(128)S(1)}, u32[]{:S(2)}) copy-start(f32[32]{0:T(128)S(1)} %convert_element_type.120) | copy-start | bytes 388
  155.1 23.1 %copy-start.44 = (f32[2]{0:T(128)}, f32[2]{0:T(128)S(1)}, u32[]{:S(2)}) copy-start(f32[2]{0:T(128)S(1)} %dynamic_slice.118) | copy-start | bytes 28
  157.2 23.7 %copy-start.23 = (bf16[128,16,2]{0,2,1:T(2,128)(2,1)}, bf16[128,16,2]{0,2,1:T(2,128)(2,1)S(1)}, u32[]{:S(2)}) copy-start(bf16[128,16,2]{0,2,1:T(2,128)(2,1)S(1)} %all-to-all-done) | copy-start | bytes 24580
  157.2 20.9 %all-to-all-start.1 = ((bf16[128,16,128]{2,0,1:T(8,128)(2,1)}), bf16[128,16,128]{2,0,1:T(8,128)(2,1)S(1)}, u32[]{:S(2)}, u32[]{:S(2)}) async-start(bf16[128,16,128]{2,0,1:T(8,128)(2,1)} %copy.109), calls=%async_computation.1 | async-start | bytes 1048576 | tf_op jit(solution)/shard_map/all_to_all | solution.py:144
  164.4 16.5 %copy-start.46 = (f32[128]{0:T(128)}, f32[128]{0:T(128)S(1)}, u32[]{:S(2)}) copy-start(f32[128]{0:T(128)S(1)} %get-tuple-element.796) | copy-start | bytes 1540
  164.4 16.5 %copy-start.48 = (f32[128]{0:T(128)}, f32[128]{0:T(128)S(1)}, u32[]{:S(2)}) copy-start(f32[128]{0:T(128)S(1)} %get-tuple-element.797) | copy-start | bytes 1540
  164.4 16.5 %copy-start.50 = (f32[128]{0:T(128)}, f32[128]{0:T(128)S(1)}, u32[]{:S(2)}) copy-start(f32[128]{0:T(128)S(1)} %get-tuple-element.798) | copy-start | bytes 1540
  164.4 16.5 %copy-start.52 = (f32[128]{0:T(128)}, f32[128]{0:T(128)S(1)}, u32[]{:S(2)}) copy-start(f32[128]{0:T(128)S(1)} %get-tuple-element.799) | copy-start | bytes 1540
  164.5 21.4 %copy-start.35 = (f32[1,256]{1,0:T(1,128)}, f32[1,256]{1,0:T(1,128)S(1)}, u32[]{:S(2)}) copy-start(f32[1,256]{1,0:T(1,128)S(1)} %get-tuple-element.792) | copy-start | bytes 3076
  164.5 21.4 %copy-start.37 = (f32[1,256]{1,0:T(1,128)}, f32[1,256]{1,0:T(1,128)S(1)}, u32[]{:S(2)}) copy-start(f32[1,256]{1,0:T(1,128)S(1)} %get-tuple-element.793) | copy-start | bytes 3076
  164.5 21.4 %copy-start.39 = (f32[1,256]{1,0:T(1,128)}, f32[1,256]{1,0:T(1,128)S(1)}, u32[]{:S(2)}) copy-start(f32[1,256]{1,0:T(1,128)S(1)} %get-tuple-element.794) | copy-start | bytes 3076
  164.5 21.4 %copy-start.41 = (f32[1,256]{1,0:T(1,128)}, f32[1,256]{1,0:T(1,128)S(1)}, u32[]{:S(2)}) copy-start(f32[1,256]{1,0:T(1,128)S(1)} %get-tuple-element.795) | copy-start | bytes 3076
  164.5 16.4 %copy-start.19 = (f32[128,16,2]{0,2,1:T(2,128)}, f32[128,16,2]{0,2,1:T(2,128)S(1)}, u32[]{:S(2)}) copy-start(f32[128,16,2]{0,2,1:T(2,128)S(1)} %convert_element_type.151) | copy-start | bytes 49156
  180.9 97.4 %copy-start.2 = (f32[2048,128]{1,0:T(8,128)}, f32[2048,128]{1,0:T(8,128)S(1)}, u32[]{:S(2)}) copy-start(f32[2048,128]{1,0:T(8,128)S(1)} %get-tuple-element.765) | copy-start | bytes 3145732
  280.5 19.6 %all-to-all-start.2 = ((bf16[16,128,128]{2,1,0:T(8,128)(2,1)}), bf16[16,128,128]{2,1,0:T(8,128)(2,1)S(1)}, u32[]{:S(2)}, u32[]{:S(2)}) async-start(bf16[16,128,128]{2,1,0:T(8,128)(2,1)} %bitcast.20), calls=%async_computation.2 | async-start | bytes 1048576 | tf_op jit(solution)/shard_map/all_to_all | solution.py:174
  289.9 16.3 %copy-start.16 = (f32[2048]{0:T(1024)}, f32[2048]{0:T(1024)S(1)}, u32[]{:S(2)}) copy-start(f32[2048]{0:T(1024)S(1)} %convert_element_type.133) | copy-start | bytes 24580
  311.2 18.6 %all-to-all-start.3 = ((bf16[128,16,128]{2,0,1:T(8,128)(2,1)}), bf16[128,16,128]{2,0,1:T(8,128)(2,1)S(1)}, u32[]{:S(2)}, u32[]{:S(2)}) async-start(bf16[128,16,128]{2,0,1:T(8,128)(2,1)} %copy.118), calls=%async_computation.3 | async-start | bytes 1048576 | tf_op jit(solution)/shard_map/all_to_all | solution.py:190
  315.3 271.9 %reduce-scatter.10.cloned.1.call-start = ((), (), s32[]{:S(2)}) async-start(), calls=%async_computation.16 | async-start | bytes 1114112
  354.5 7.7 copy-start.15
  376.2 7.7 copy-start.15
  397.9 7.7 copy-start.15
  419.6 7.7 copy-start.15
  441.3 7.7 copy-start.15
  463.0 7.7 copy-start.15
  484.7 7.7 copy-start.15
  506.4 7.7 copy-start.15
  529.1 208.4 %reduce-scatter.8.cloned.1.call-start = ((), (), s32[]{:S(2)}) async-start(), calls=%async_computation.14 | async-start | bytes 8650752 | tf_op jit(solution)/shard_map/reduce_scatter | solution.py:237
  546.2 42.0 %copy-start.14 = (bf16[128,2048]{0,1:T(8,128)(2,1)S(1)}, bf16[128,2048]{0,1:T(8,128)(2,1)}, u32[]{:S(2)}) copy-start(bf16[128,2048]{0,1:T(8,128)(2,1)} %get-tuple-element.779) | copy-start | bytes 1572868
  546.2 42.0 %copy-start.28 = (f32[128]{0:T(128)S(1)}, f32[128]{0:T(128)}, u32[]{:S(2)}) copy-start(f32[128]{0:T(128)} %copy-done.27) | copy-start | bytes 1540
  546.2 21.5 %all-to-all-start.4 = ((bf16[16,128,128]{2,1,0:T(8,128)(2,1)}), bf16[16,128,128]{2,1,0:T(8,128)(2,1)S(1)}, u32[]{:S(2)}, u32[]{:S(2)}) async-start(bf16[16,128,128]{2,1,0:T(8,128)(2,1)} %bitcast.441), calls=%async_computation.4 | async-start | bytes 1048576 | tf_op jit(solution)/shard_map/all_to_all | solution.py:206
  567.6 20.5 %all-to-all-start.5 = ((bf16[16,128,2]{1,2,0:T(2,128)(2,1)}), bf16[16,128,2]{1,2,0:T(2,128)(2,1)S(1)}, u32[]{:S(2)}, u32[]{:S(2)}) async-start(bf16[16,128,2]{1,2,0:T(2,128)(2,1)} %fusion.124), calls=%async_computation.5 | async-start | bytes 16384 | tf_op jit(solution)/shard_map/all_to_all | solution.py:209
  573.0 359.4 %reduce-scatter.6.cloned.1.call-start = ((), (), s32[]{:S(2)}) async-start(), calls=%async_computation.12 | async-start | bytes 18923520 | tf_op jit(solution)/shard_map/reduce_scatter | solution.py:236
  596.2 399.6 %all-gather.16.cloned.1.call-start = ((), (), s32[]{:S(2)}) async-start(), calls=%async_computation.15 | async-start | bytes 4456448 | tf_op jit(solution)/shard_map/all_gather | solution.py:241
  737.6 333.8 %all-gather.14.cloned.1.call-start = ((), (), s32[]{:S(2)}) async-start(), calls=%async_computation.13 | async-start | bytes 9748480 | tf_op jit(solution)/shard_map/all_gather | solution.py:240
  938.3 55.8 %copy-start.66 = (f32[128]{0:T(128)S(1)}, f32[128]{0:T(128)}, u32[]{:S(2)}) copy-start(f32[128]{0:T(128)} %copy-done.65) | copy-start | bytes 1540
  938.3 56.5 %copy-start.13 = (bf16[128,1024]{1,0:T(8,128)(2,1)S(1)}, bf16[128,1024]{1,0:T(8,128)(2,1)}, u32[]{:S(2)}) copy-start(bf16[128,1024]{1,0:T(8,128)(2,1)} %param.25) | copy-start | bytes 786436
  (85 other events, 310.9 us)
Sparse Core Ops, SparseCore 0:
  9.6 115.6 all-gather.7
  132.3 39.7 all-gather.9
  173.7 57.0 all-gather.11
  529.2 57.9 reduce-scatter.9
  590.0 147.4 reduce-scatter.7
  739.8 192.5 reduce-scatter.5
  934.6 56.0 all-gather.15
  993.0 78.3 all-gather.13
where the time goes:
time: 1100 us; the launch traced here: 1090 us
  waiting for transfers between devices  592 us (54%)
  matrix products  155 us (14%)
  local copies, waits for them, and re-layouts  116 us (11%)
  other arithmetic  111 us (10%)
  blocking collectives  70.2 us (6%)
  starting transfers between devices  31.6 us (3%)
  between operations  16.1 us (1%)
    reduce_scatter x1, waiting for transfers between devices, local(): lax.psum_scatter(in_grad, ('dp', 'seq'), scatter_dimension=0, tiled=True)  195 us
    reduce_scatter x1, waiting for transfers between devices, local(): lax.psum_scatter(out_grad, ('dp', 'seq'), scatter_dimension=0, tiled=True)  141 us
    all_gather x1, waiting for transfers between devices, local(): lax.all_gather(in_weight, 'dp', axis=0, tiled=True)  112 us
    all_gather x1, waiting for transfers between devices, local(): lax.all_gather(in_part, 'seq', axis=0, tiled=True)  75.6 us
    dot_general x24, matrix products, one_block(): inside = jnp.einsum('hts,shp->thp', weights, val_blk, precision=highest)  48.4 us
    psum x1, blocking collectives, local(): lax.psum((gain_grad, taps_grad, offset_grad, shift_grad, rates_grad, skip...  47 us
    another operation x50, other arithmetic  37.1 us
    dot_general x32, matrix products, one_block(): scores = jnp.dot(query_blk, key_blk.T, precision=highest)  31.6 us
  transfers between devices with their start and end apart: 14, of which 9 were waited for; matrix products, arithmetic and copies ran while one was open for 14% of the time, Pallas kernels for 0%

commit v1 on v0

--- a/solution.py
+++ b/solution.py
@@ -6,6 +6,17 @@
 BLOCK = 256
 epsilon = 1e-05
 highest = lax.Precision.HIGHEST
+
+
+def collect(x, axis, dim):
+    ways = lax.axis_size(axis)
+    pieces = [x]
+    for far in range(1, ways):
+        pieces.append(
+            lax.ppermute(pieces[far - 1], axis, [(d, (d - 1) % ways) for d in range(ways)])
+        )
+    line = jnp.concatenate(pieces, axis=dim)
+    return jnp.roll(line, lax.axis_index(axis) * x.shape[dim], axis=dim)
 
 
 def front_norm(values, gain):
@@ -237,7 +248,7 @@
         lax.psum_scatter(out_grad, ("dp", "seq"), scatter_dimension=0, tiled=True),
     )
     in_shard, out_shard = (
-        lax.all_gather(in_part, "seq", axis=0, tiled=True),
+        collect(in_part, "seq", 0),
         lax.all_gather(out_part, "seq", axis=0, tiled=True),
     )
     gain_all, taps_all, offset_all, shift_all, rates_all, skip_all, gate_all = lax.psum(

time: 1100 us -> 1060 us (0.964)
  waiting for transfers between devices: 592 us -> 466 us
  starting transfers between devices: 31.6 us -> 103 us
    reduce_scatter x1, waiting for transfers between devices: 141 us -> 0.02 us  [local(): lax.psum_scatter(out_grad, ('dp', 'seq'), scatter_dimension=0, tiled=True)]
    ppermute x0 -> x15, waiting for transfers between devices: none -> 107 us  [collect(): lax.ppermute(pieces[far - 1], axis, [(d, (d - 1) % ways) for d in range(w...]
    all_gather x1 -> x0, waiting for transfers between devices: 75.6 us -> none  [local(): lax.all_gather(in_part, 'seq', axis=0, tiled=True)]
    ppermute x0 -> x15, starting transfers between devices: none -> 72.1 us  [collect(): lax.ppermute(pieces[far - 1], axis, [(d, (d - 1) % ways) for d in range(w...]
    reduce_scatter x1, waiting for transfers between devices: 195 us -> 181 us  [local(): lax.psum_scatter(in_grad, ('dp', 'seq'), scatter_dimension=0, tiled=True)]
    unnamed x157 -> x178, local copies, waits for them, and re-layouts: 30.9 us -> 32.4 us
  transfers between devices with their start and end apart: 14 -> 28, of which waited for: 9 -> 22; matrix products, arithmetic and copies ran while one was open for 14% -> 33% of each run, Pallas kernels for 0% -> 0%
where the time goes in v1:
time: 1060 us; the launch traced here: 1050 us
  waiting for transfers between devices  466 us (44%)
  matrix products  163 us (15%)
  local copies, waits for them, and re-layouts  123 us (12%)
  other arithmetic  110 us (10%)
  starting transfers between devices  103 us (10%)
  blocking collectives  64.8 us (6%)
  between operations  16.2 us (2%)
    reduce_scatter x1, waiting for transfers between devices, local(): lax.psum_scatter(in_grad, ('dp', 'seq'), scatter_dimension=0, tiled=True)  181 us
    all_gather x1, waiting for transfers between devices, local(): lax.all_gather(in_weight, 'dp', axis=0, tiled=True)  112 us
    ppermute x15, waiting for transfers between devices, collect(): lax.ppermute(pieces[far - 1], axis, [(d, (d - 1) % ways) for d in range(w...  107 us
    ppermute x15, starting transfers between devices, collect(): lax.ppermute(pieces[far - 1], axis, [(d, (d - 1) % ways) for d in range(w...  72.1 us
    dot_general x24, matrix products, one_block(): inside = jnp.einsum('hts,shp->thp', weights, val_blk, precision=highest)  48.5 us
    psum x1, blocking collectives, local(): lax.psum((gain_grad, taps_grad, offset_grad, shift_grad, rates_grad, skip...  41.5 us
    another operation x50, other arithmetic  37.1 us
    unnamed x178, local copies, waits for them, and re-layouts  32.4 us
  transfers between devices with their start and end apart: 28, of which 22 were waited for; matrix products, arithmetic and copies ran while one was open for 33% of the time, Pallas kernels for 0%

profile of v1, /device:TPU:0, one launch (start us, length us, event | category | flops | bytes accessed | tf_op | source)
XLA Modules:
  0.0 1047.8 jit_solution(6792528382339815030)
XLA Ops:
  8.0 5.3 all-gather
  13.4 111.9 %all-gather.7.cloned.1.call-done = bf16[1024,4384]{0,1:T(8,128)(2,1)} async-done(((bf16[512,4384]{0,1:T(8,128)(2,1)}), bf16[1024,4384]{0,1:T(8,128)(2,1)}) %all-gather.7.cloned.1.call-update) | async-done | bytes 8978448 | tf_op jit(solution)/shard_map/all_gather | solution.py:130
  125.3 6.2 convolution_convert_fusion
  138.0 5.6 all-to-all-start
  145.7 4.9 all-reduce.26
  157.3 6.5 all-to-all-start.1
  165.4 12.8 %all-to-all-done.1 = bf16[128,16,128]{2,0,1:T(8,128)(2,1)S(1)} async-done(((bf16[128,16,128]{2,0,1:T(8,128)(2,1)}), bf16[128,16,128]{2,0,1:T(8,128)(2,1)S(1)}, u32[]{:S(2)}, u32[]{:S(2)}) %all-to-all-start.1) | async-done | bytes 524320 | tf_op jit(solution)/shard_map/all_to_all | solution.py:155
  195.8 75.2 %while.44 = (s32[]{:T(128)}, f32[2,64,128]{2,1,0:T(8,128)S(1)}, f32[8,256,2,64]{1,3,2,0:T(8,128)}, f32[8,2,64,128]{3,2,1,0:T(8,128)}, f32[8,256,2]{1,2,0:T(2,128...) while((s32[]{:T(128)}, f32[2,64,128]{2,1,0:T(8,128)S(1)}, ...), condition=%wide.region_4.5_spmd.clone.clone, body=%wide.region_1.4_spmd.clone.clone.sunk | while | flops 302892544 | bytes 2142528 | solution.py:78
  280.5 5.0 all-to-all-start.2
  289.9 10.1 all-to-all-done.2
  315.9 5.6 fusion.131
  321.8 7.9 all-to-all-done.3
  341.9 179.1 %while.43 = (s32[]{:T(128)}, f32[2]{0:T(128)}, f32[2,64,128]{2,1,0:T(8,128)S(1)}, f32[8,256,2,64]{1,3,2,0:T(8,128)}, f32[8,256,2]{1,2,0:T(2,128)}, /*index=5*/f3...) while((s32[]{:T(128)}, f32[2]{0:T(128)}, ...), condition=%wide.region_20.21_spmd.clone, body=%wide.region_7.20_spmd.clone.sunk | while | flops 758179328 | bytes 7913312 | solution.py:78
  552.0 14.7 %all-to-all-done.4 = bf16[16,128,128]{2,1,0:T(8,128)(2,1)S(1)} async-done(((bf16[16,128,128]{2,1,0:T(8,128)(2,1)}), bf16[16,128,128]{2,1,0:T(8,128)(2,1)S(1)}, u32[]{:S(2)}, u32[]{:S(2)}) %all-to-all-start.4) | async-done | bytes 524320 | tf_op jit(solution)/shard_map/all_to_all | solution.py:217
  566.7 5.0 all-to-all-start.5
  572.0 18.9 %reduce-scatter.10.cloned.1.call-done = bf16[128,256]{1,0:T(8,128)(2,1)} async-done(((bf16[2048,256]{1,0:T(8,128)(2,1)}), bf16[128,256]{1,0:T(8,128)(2,1)}) %reduce-scatter.10.cloned.1.call-update) | async-done | bytes 65552
  591.9 9.0 fusion.110
  607.3 5.2 fusion.106
  612.4 41.5 %all-reduce.25 = (f32[1024]{0:T(1024)S(1)}, f32[4,2304]{1,0:T(4,128)S(1)}, f32[2304]{0:T(1024)S(1)}, f32[32]{0:T(128)S(1)}, f32[32]{0:T(128)S(1)}, /*index=5*/f32[32]{0:T(128)S(1)}, f32[2048]{0:T(1024)S(1)}) all-reduce(f32[1024]{0:T(1024)S(1)} %get-tuple-element.697, ...), channel_id=1, replica_groups=mesh['dp'=2,'seq'=16] {'dp','seq'}, use_global_device_ids=true, to_apply=%region_24.25 | all-reduce | flops 14688 | bytes 117504 | tf_op jit(solution)/shard_map/psum | solution.py:254
  659.3 181.4 %reduce-scatter.6.cloned.1.call-done = f32[32,4384]{1,0:T(8,128)} async-done(((f32[1024,4384]{1,0:T(8,128)}), f32[32,4384]{1,0:T(8,128)}) %reduce-scatter.6.cloned.1.call-update) | async-done | bytes 561168 | tf_op jit(solution)/shard_map/reduce_scatter | solution.py:247
  840.7 7.5 collective-permute-start
  849.3 6.4 collective-permute-done
  860.2 7.2 collective-permute-done.1
  872.1 7.2 collective-permute-done.2
  879.2 4.6 collective-permute-start.3
  883.9 7.2 collective-permute-done.3
  891.1 4.6 collective-permute-start.4
  895.7 7.2 collective-permute-done.4
  902.9 4.6 collective-permute-start.5
  907.6 7.2 collective-permute-done.5
  914.7 4.6 collective-permute-start.6
  919.4 7.2 collective-permute-done.6
  926.6 4.6 collective-permute-start.7
  931.2 7.2 collective-permute-done.7
  938.4 4.9 collective-permute-start.8
  943.3 7.2 collective-permute-done.8
  950.5 4.6 collective-permute-start.9
  955.1 7.2 collective-permute-done.9
  962.3 4.6 collective-permute-start.10
  967.0 7.2 collective-permute-done.10
  974.2 4.6 collective-permute-start.11
  978.8 7.2 collective-permute-done.11
  986.0 4.6 collective-permute-start.12
  990.6 7.2 collective-permute-done.12
  1002.5 7.2 collective-permute-done.13
  1014.3 7.2 collective-permute-done.14
  1026.4 9.4 copy.130
  1035.9 4.8 copy.284
  (820 shorter events, 397.6 us)
Async XLA Ops:
  7.2 118.1 %all-gather.7.cloned.1.call-start = ((), (), s32[]{:S(2)}) async-start(), calls=%async_computation.9 | async-start | bytes 13467648 | tf_op jit(solution)/shard_map/all_gather | solution.py:130
  7.9 176.5 %all-gather.9.cloned.1.call-start = ((), (), s32[]{:S(2)}) async-start(), calls=%async_computation.10 | async-start | bytes 1114112 | tf_op jit(solution)/shard_map/all_gather | solution.py:158
  13.4 118.1 %copy-start.59 = (f32[128]{0:T(128)}, f32[128]{0:T(128)S(1)}, u32[]{:S(2)}) copy-start(f32[128]{0:T(128)S(1)} %fusion.108) | copy-start | bytes 1540
  13.4 118.1 %copy-start.25 = (f32[128]{0:T(128)}, f32[128]{0:T(128)S(1)}, u32[]{:S(2)}) copy-start(f32[128]{0:T(128)S(1)} %fusion.126) | copy-start | bytes 1540
  125.3 19.9 %copy-start.67 = (bf16[16]{0:T(256)(128)(2,1)S(1)}, bf16[16]{0:T(256)(128)(2,1)}, u32[]{:S(2)}) copy-start(bf16[16]{0:T(256)(128)(2,1)} %param.22) | copy-start | bytes 100
  125.3 20.1 %copy-start.68 = (bf16[16]{0:T(256)(128)(2,1)S(1)}, bf16[16]{0:T(256)(128)(2,1)}, u32[]{:S(2)}) copy-start(bf16[16]{0:T(256)(128)(2,1)} %param.21) | copy-start | bytes 100
  125.3 25.3 %copy-start.41 = (bf16[4,1152]{1,0:T(4,128)(2,1)S(1)}, bf16[4,1152]{1,0:T(4,128)(2,1)}, u32[]{:S(2)}) copy-start(bf16[4,1152]{1,0:T(4,128)(2,1)} %param.18) | copy-start | bytes 27652
  131.5 46.8 %copy-start.7 = (bf16[128,4384]{0,1:T(8,128)(2,1)}, bf16[128,4384]{0,1:T(8,128)(2,1)S(1)}, u32[]{:S(2)}) copy-start(bf16[128,4384]{0,1:T(8,128)(2,1)S(1)} %convolution_convert_fusion) | copy-start | bytes 3366916
  132.3 169.6 %all-gather.11.cloned.1.call-start = ((), (), s32[]{:S(2)}) async-start(), calls=%async_computation.11 | async-start | bytes 6291456 | tf_op jit(solution)/shard_map/all_gather | solution.py:137
  138.0 19.3 %all-to-all-start = ((bf16[128,16,2]{0,2,1:T(2,128)(2,1)}), bf16[128,16,2]{0,2,1:T(2,128)(2,1)S(1)}, u32[]{:S(2)}, u32[]{:S(2)}) async-start(bf16[128,16,2]{0,2,1:T(2,128)(2,1)} %bitcast.3), calls=%async_computation | async-start | bytes 16384 | tf_op jit(solution)/shard_map/all_to_all | solution.py:156
  150.6 30.4 %copy-start.63 = (f32[32]{0:T(128)}, f32[32]{0:T(128)S(1)}, u32[]{:S(2)}) copy-start(f32[32]{0:T(128)S(1)} %convert_element_type.120) | copy-start | bytes 388
  155.2 25.9 %copy-start.42 = (f32[2]{0:T(128)}, f32[2]{0:T(128)S(1)}, u32[]{:S(2)}) copy-start(f32[2]{0:T(128)S(1)} %dynamic_slice.122) | copy-start | bytes 28
  157.2 25.0 %copy-start.21 = (bf16[128,16,2]{0,2,1:T(2,128)(2,1)}, bf16[128,16,2]{0,2,1:T(2,128)(2,1)S(1)}, u32[]{:S(2)}) copy-start(bf16[128,16,2]{0,2,1:T(2,128)(2,1)S(1)} %all-to-all-done) | copy-start | bytes 24580
  157.3 21.0 %all-to-all-start.1 = ((bf16[128,16,128]{2,0,1:T(8,128)(2,1)}), bf16[128,16,128]{2,0,1:T(8,128)(2,1)S(1)}, u32[]{:S(2)}, u32[]{:S(2)}) async-start(bf16[128,16,128]{2,0,1:T(8,128)(2,1)} %copy.109), calls=%async_computation.1 | async-start | bytes 1048576 | tf_op jit(solution)/shard_map/all_to_all | solution.py:155
  164.5 19.8 %copy-start.46 = (f32[128]{0:T(128)}, f32[128]{0:T(128)S(1)}, u32[]{:S(2)}) copy-start(f32[128]{0:T(128)S(1)} %get-tuple-element.797) | copy-start | bytes 1540
  164.6 21.4 %copy-start.33 = (f32[1,256]{1,0:T(1,128)}, f32[1,256]{1,0:T(1,128)S(1)}, u32[]{:S(2)}) copy-start(f32[1,256]{1,0:T(1,128)S(1)} %get-tuple-element.792) | copy-start | bytes 3076
  164.6 21.4 %copy-start.35 = (f32[1,256]{1,0:T(1,128)}, f32[1,256]{1,0:T(1,128)S(1)}, u32[]{:S(2)}) copy-start(f32[1,256]{1,0:T(1,128)S(1)} %get-tuple-element.793) | copy-start | bytes 3076
  164.6 21.4 %copy-start.37 = (f32[1,256]{1,0:T(1,128)}, f32[1,256]{1,0:T(1,128)S(1)}, u32[]{:S(2)}) copy-start(f32[1,256]{1,0:T(1,128)S(1)} %get-tuple-element.794) | copy-start | bytes 3076
  164.6 21.4 %copy-start.39 = (f32[1,256]{1,0:T(1,128)}, f32[1,256]{1,0:T(1,128)S(1)}, u32[]{:S(2)}) copy-start(f32[1,256]{1,0:T(1,128)S(1)} %get-tuple-element.795) | copy-start | bytes 3076
  181.0 97.3 %copy-start.2 = (f32[2048,128]{1,0:T(8,128)}, f32[2048,128]{1,0:T(8,128)S(1)}, u32[]{:S(2)}) copy-start(f32[2048,128]{1,0:T(8,128)S(1)} %get-tuple-element.765) | copy-start | bytes 3145732
  280.5 19.5 %all-to-all-start.2 = ((bf16[16,128,128]{2,1,0:T(8,128)(2,1)}), bf16[16,128,128]{2,1,0:T(8,128)(2,1)S(1)}, u32[]{:S(2)}, u32[]{:S(2)}) async-start(bf16[16,128,128]{2,1,0:T(8,128)(2,1)} %bitcast.20), calls=%async_computation.2 | async-start | bytes 1048576 | tf_op jit(solution)/shard_map/all_to_all | solution.py:185
  289.9 26.0 %copy-start.14 = (f32[2048]{0:T(1024)}, f32[2048]{0:T(1024)S(1)}, u32[]{:S(2)}) copy-start(f32[2048]{0:T(1024)S(1)} %convert_element_type.133) | copy-start | bytes 24580
  311.1 18.6 %all-to-all-start.3 = ((bf16[128,16,128]{2,0,1:T(8,128)(2,1)}), bf16[128,16,128]{2,0,1:T(8,128)(2,1)S(1)}, u32[]{:S(2)}, u32[]{:S(2)}) async-start(bf16[128,16,128]{2,0,1:T(8,128)(2,1)} %copy.118), calls=%async_computation.3 | async-start | bytes 1048576 | tf_op jit(solution)/shard_map/all_to_all | solution.py:201
  315.2 219.3 %reduce-scatter.8.cloned.1.call-start = ((), (), s32[]{:S(2)}) async-start(), calls=%async_computation.13 | async-start | bytes 8650752 | tf_op jit(solution)/shard_map/reduce_scatter | solution.py:248
  321.6 269.3 %reduce-scatter.10.cloned.1.call-start = ((), (), s32[]{:S(2)}) async-start(), calls=%async_computation.15 | async-start | bytes 1114112
  534.2 125.1 %all-gather.13.cloned.1.call-start = ((), (), s32[]{:S(2)}) async-start(), calls=%async_computation.14 | async-start | bytes 4456448 | tf_op jit(solution)/shard_map/all_gather | solution.py:252
  545.9 45.9 %copy-start.26 = (f32[128]{0:T(128)S(1)}, f32[128]{0:T(128)}, u32[]{:S(2)}) copy-start(f32[128]{0:T(128)} %copy-done.25) | copy-start | bytes 1540
  547.1 19.6 %all-to-all-start.4 = ((bf16[16,128,128]{2,1,0:T(8,128)(2,1)}), bf16[16,128,128]{2,1,0:T(8,128)(2,1)S(1)}, u32[]{:S(2)}, u32[]{:S(2)}) async-start(bf16[16,128,128]{2,1,0:T(8,128)(2,1)} %bitcast.441), calls=%async_computation.4 | async-start | bytes 1048576 | tf_op jit(solution)/shard_map/all_to_all | solution.py:217
  566.7 25.2 %all-to-all-start.5 = ((bf16[16,128,2]{1,2,0:T(2,128)(2,1)}), bf16[16,128,2]{1,2,0:T(2,128)(2,1)S(1)}, u32[]{:S(2)}, u32[]{:S(2)}) async-start(bf16[16,128,2]{1,2,0:T(2,128)(2,1)} %fusion.124), calls=%async_computation.5 | async-start | bytes 16384 | tf_op jit(solution)/shard_map/all_to_all | solution.py:220
  571.6 269.0 %reduce-scatter.6.cloned.1.call-start = ((), (), s32[]{:S(2)}) async-start(), calls=%async_computation.12 | async-start | bytes 18923520 | tf_op jit(solution)/shard_map/reduce_scatter | solution.py:247
  607.2 50.4 %copy-start.60 = (f32[128]{0:T(128)S(1)}, f32[128]{0:T(128)}, u32[]{:S(2)}) copy-start(f32[128]{0:T(128)} %copy-done.59) | copy-start | bytes 1540
  607.3 51.0 %copy-start.11 = (bf16[128,1024]{1,0:T(8,128)(2,1)S(1)}, bf16[128,1024]{1,0:T(8,128)(2,1)}, u32[]{:S(2)}) copy-start(bf16[128,1024]{1,0:T(8,128)(2,1)} %param.25) | copy-start | bytes 786436
  840.7 15.0 %collective-permute-start = (f32[32,4384]{1,0:T(8,128)}, f32[32,4384]{1,0:T(8,128)S(1)}, u32[]{:S(2)}, u32[]{:S(2)}) collective-permute-start(f32[32,4384]{1,0:T(8,128)} %reduce-scatter.6.cloned.1.call-done), channel_id=1, source_target_pairs={{0,15},{1,0},{2,1},{3,2},{4,3},{5,4},{6,5},{7,6},{8,7},{9,8},{10,9... | collective-permute-start | bytes 1683464 | tf_op jit(solution)/shard_map/ppermute | solution.py:16
  855.7 11.7 %collective-permute-start.1 = (f32[32,4384]{1,0:T(8,128)S(1)}, f32[32,4384]{1,0:T(8,128)S(1)}, u32[]{:S(2)}, u32[]{:S(2)}) collective-permute-start(f32[32,4384]{1,0:T(8,128)S(1)} %collective-permute-done), channel_id=1, source_target_pairs={{0,15},{1,0},{2,1},{3,2},{4,3},{5,4},{6,5},{7,6},{8,7},{9,8},{10,9... | collective-permute-start | bytes 1683464 | tf_op jit(solution)/shard_map/ppermute | solution.py:16
  867.4 11.8 %collective-permute-start.2 = (f32[32,4384]{1,0:T(8,128)S(1)}, f32[32,4384]{1,0:T(8,128)S(1)}, u32[]{:S(2)}, u32[]{:S(2)}) collective-permute-start(f32[32,4384]{1,0:T(8,128)S(1)} %collective-permute-done.1), channel_id=1, source_target_pairs={{0,15},{1,0},{2,1},{3,2},{4,3},{5,4},{6,5},{7,6},{8,7},{9,8},{10,9... | collective-permute-start | bytes 1683464 | tf_op jit(solution)/shard_map/ppermute | solution.py:16
  879.2 11.8 %collective-permute-start.3 = (f32[32,4384]{1,0:T(8,128)S(1)}, f32[32,4384]{1,0:T(8,128)S(1)}, u32[]{:S(2)}, u32[]{:S(2)}) collective-permute-start(f32[32,4384]{1,0:T(8,128)S(1)} %collective-permute-done.2), channel_id=1, source_target_pairs={{0,15},{1,0},{2,1},{3,2},{4,3},{5,4},{6,5},{7,6},{8,7},{9,8},{10,9... | collective-permute-start | bytes 1683464 | tf_op jit(solution)/shard_map/ppermute | solution.py:16
  891.1 11.8 %collective-permute-start.4 = (f32[32,4384]{1,0:T(8,128)S(1)}, f32[32,4384]{1,0:T(8,128)S(1)}, u32[]{:S(2)}, u32[]{:S(2)}) collective-permute-start(f32[32,4384]{1,0:T(8,128)S(1)} %collective-permute-done.3), channel_id=1, source_target_pairs={{0,15},{1,0},{2,1},{3,2},{4,3},{5,4},{6,5},{7,6},{8,7},{9,8},{10,9... | collective-permute-start | bytes 1683464 | tf_op jit(solution)/shard_map/ppermute | solution.py:16
  902.9 11.8 %collective-permute-start.5 = (f32[32,4384]{1,0:T(8,128)S(1)}, f32[32,4384]{1,0:T(8,128)S(1)}, u32[]{:S(2)}, u32[]{:S(2)}) collective-permute-start(f32[32,4384]{1,0:T(8,128)S(1)} %collective-permute-done.4), channel_id=1, source_target_pairs={{0,15},{1,0},{2,1},{3,2},{4,3},{5,4},{6,5},{7,6},{8,7},{9,8},{10,9... | collective-permute-start | bytes 1683464 | tf_op jit(solution)/shard_map/ppermute | solution.py:16
  914.7 11.8 %collective-permute-start.6 = (f32[32,4384]{1,0:T(8,128)S(1)}, f32[32,4384]{1,0:T(8,128)S(1)}, u32[]{:S(2)}, u32[]{:S(2)}) collective-permute-start(f32[32,4384]{1,0:T(8,128)S(1)} %collective-permute-done.5), channel_id=1, source_target_pairs={{0,15},{1,0},{2,1},{3,2},{4,3},{5,4},{6,5},{7,6},{8,7},{9,8},{10,9... | collective-permute-start | bytes 1683464 | tf_op jit(solution)/shard_map/ppermute | solution.py:16
  926.6 11.8 %collective-permute-start.7 = (f32[32,4384]{1,0:T(8,128)S(1)}, f32[32,4384]{1,0:T(8,128)S(1)}, u32[]{:S(2)}, u32[]{:S(2)}) collective-permute-start(f32[32,4384]{1,0:T(8,128)S(1)} %collective-permute-done.6), channel_id=1, source_target_pairs={{0,15},{1,0},{2,1},{3,2},{4,3},{5,4},{6,5},{7,6},{8,7},{9,8},{10,9... | collective-permute-start | bytes 1683464 | tf_op jit(solution)/shard_map/ppermute | solution.py:16
  938.4 12.1 %collective-permute-start.8 = (f32[32,4384]{1,0:T(8,128)S(1)}, f32[32,4384]{1,0:T(8,128)S(1)}, u32[]{:S(2)}, u32[]{:S(2)}) collective-permute-start(f32[32,4384]{1,0:T(8,128)S(1)} %collective-permute-done.7), channel_id=1, source_target_pairs={{0,15},{1,0},{2,1},{3,2},{4,3},{5,4},{6,5},{7,6},{8,7},{9,8},{10,9... | collective-permute-start | bytes 1683464 | tf_op jit(solution)/shard_map/ppermute | solution.py:16
  943.3 78.2 %copy-start.12 = (f32[32,4384]{1,0:T(8,128)S(1)}, f32[32,4384]{1,0:T(8,128)}, u32[]{:S(2)}) copy-start(f32[32,4384]{1,0:T(8,128)} %reduce-scatter.6.cloned.1.call-done) | copy-start | bytes 1683460
  950.5 11.8 %collective-permute-start.9 = (f32[32,4384]{1,0:T(8,128)S(1)}, f32[32,4384]{1,0:T(8,128)S(1)}, u32[]{:S(2)}, u32[]{:S(2)}) collective-permute-start(f32[32,4384]{1,0:T(8,128)S(1)} %collective-permute-done.8), channel_id=1, source_target_pairs={{0,15},{1,0},{2,1},{3,2},{4,3},{5,4},{6,5},{7,6},{8,7},{9,8},{10,9... | collective-permute-start | bytes 1683464 | tf_op jit(solution)/shard_map/ppermute | solution.py:16
  962.3 11.8 %collective-permute-start.10 = (f32[32,4384]{1,0:T(8,128)S(1)}, f32[32,4384]{1,0:T(8,128)S(1)}, u32[]{:S(2)}, u32[]{:S(2)}) collective-permute-start(f32[32,4384]{1,0:T(8,128)S(1)} %collective-permute-done.9), channel_id=1, source_target_pairs={{0,15},{1,0},{2,1},{3,2},{4,3},{5,4},{6,5},{7,6},{8,7},{9,8},{10,9... | collective-permute-start | bytes 1683464 | tf_op jit(solution)/shard_map/ppermute | solution.py:16
  974.2 11.8 %collective-permute-start.11 = (f32[32,4384]{1,0:T(8,128)S(1)}, f32[32,4384]{1,0:T(8,128)S(1)}, u32[]{:S(2)}, u32[]{:S(2)}) collective-permute-start(f32[32,4384]{1,0:T(8,128)S(1)} %collective-permute-done.10), channel_id=1, source_target_pairs={{0,15},{1,0},{2,1},{3,2},{4,3},{5,4},{6,5},{7,6},{8,7},{9,8},{10,9... | collective-permute-start | bytes 1683464 | tf_op jit(solution)/shard_map/ppermute | solution.py:16
  986.0 11.8 %collective-permute-start.12 = (f32[32,4384]{1,0:T(8,128)S(1)}, f32[32,4384]{1,0:T(8,128)S(1)}, u32[]{:S(2)}, u32[]{:S(2)}) collective-permute-start(f32[32,4384]{1,0:T(8,128)S(1)} %collective-permute-done.11), channel_id=1, source_target_pairs={{0,15},{1,0},{2,1},{3,2},{4,3},{5,4},{6,5},{7,6},{8,7},{9,8},{10,9... | collective-permute-start | bytes 1683464 | tf_op jit(solution)/shard_map/ppermute | solution.py:16
  997.8 11.8 %collective-permute-start.13 = (f32[32,4384]{1,0:T(8,128)S(1)}, f32[32,4384]{1,0:T(8,128)S(1)}, u32[]{:S(2)}, u32[]{:S(2)}) collective-permute-start(f32[32,4384]{1,0:T(8,128)S(1)} %collective-permute-done.12), channel_id=1, source_target_pairs={{0,15},{1,0},{2,1},{3,2},{4,3},{5,4},{6,5},{7,6},{8,7},{9,8},{10,9... | collective-permute-start | bytes 1683464 | tf_op jit(solution)/shard_map/ppermute | solution.py:16
  1009.6 11.8 %collective-permute-start.14 = (f32[32,4384]{1,0:T(8,128)S(1)}, f32[32,4384]{1,0:T(8,128)S(1)}, u32[]{:S(2)}, u32[]{:S(2)}) collective-permute-start(f32[32,4384]{1,0:T(8,128)S(1)} %collective-permute-done.13), channel_id=1, source_target_pairs={{0,15},{1,0},{2,1},{3,2},{4,3},{5,4},{6,5},{7,6},{8,7},{9,8},{10,9... | collective-permute-start | bytes 1683464 | tf_op jit(solution)/shard_map/ppermute | solution.py:16
  (86 other events, 490.1 us)
Sparse Core Ops, SparseCore 0:
  9.6 115.6 all-gather.6
  132.4 39.6 all-gather.8
  173.7 57.0 all-gather.10
  321.7 148.8 reduce-scatter.7
  534.3 56.5 reduce-scatter.9
  593.1 50.4 all-gather.12
  646.0 194.6 reduce-scatter.5
